TPU v7x, 128 devices: a whole 4x4x4 slice. The times are simulated.
128 devices in a mesh: guide: 2 (over core), kv: 4 (over y), seq: 16 (over z, x).
Axes of the slice: x: 4, y: 4, z: 4, core: 2. Of those that a mesh axis runs over, the one named last changes fastest.
Arguments:
- hidden: bfloat16 [2, 8, 4608], P(None, None, ('guide', 'seq')), may hold values from -50 to 50
- lengths: int32 [2, 8], replicated, may hold values from 1 to 8192, as said below
- slot_owner: int32 [2, 8], replicated, may hold values from 0 to 7, each once within a row
- allowed_ids: int32 [65536], P(('kv', 'seq')), may hold values from 0 to 131071, as said below
- guidance: float32 [8], replicated, may hold values from 1 to 4
- pre_attn_gain: float32 [4608], P(('guide', 'seq')), may hold values from 0.1 to 1.9
- post_attn_gain: float32 [4608], P(('guide', 'seq')), may hold values from 0.4 to 2.1
- pre_ffw_gain: float32 [4608], P(('guide', 'seq')), may hold values from 0.1 to 1.9
- post_ffw_gain: float32 [4608], P(('guide', 'seq')), may hold values from 0.4 to 2.1
- final_gain: float32 [4608], P(('guide', 'seq')), may hold values from 0.1 to 1.9
- query_weight: bfloat16 [4608, 4096], P(('guide', 'seq'), 'kv'), may hold values from -0.09375 to 0.09375
- key_weight: bfloat16 [4608, 2048], P(('guide', 'seq'), 'kv'), may hold values from -0.09375 to 0.09375
- value_weight: bfloat16 [4608, 2048], P(('guide', 'seq'), 'kv'), may hold values from -0.09375 to 0.09375
- output_weight: bfloat16 [4096, 4608], P('kv', ('guide', 'seq')), may hold values from -1 to 1
- gate_weight: bfloat16 [4608, 36864], P(('guide', 'seq'), 'kv'), may hold values from -1 to 1
- up_weight: bfloat16 [4608, 36864], P(('guide', 'seq'), 'kv'), may hold values from -1 to 1
- down_weight: bfloat16 [36864, 4608], P('kv', ('guide', 'seq')), may hold values from -1 to 1
- embedding: bfloat16 [131072, 4608], P(('kv', 'seq'), 'guide'), may hold values from -1 to 1
- cond_keys: bfloat16 [8, 8192, 2048], P(None, ('guide', 'seq'), 'kv'), may hold values from -6 to 6
- cond_values: bfloat16 [8, 8192, 2048], P(None, ('guide', 'seq'), 'kv'), may hold values from -6 to 6
- uncond_keys: bfloat16 [8, 2048, 2048], P(None, ('guide', 'seq'), 'kv'), may hold values from -6 to 6
- uncond_values: bfloat16 [8, 2048, 2048], P(None, ('guide', 'seq'), 'kv'), may hold values from -6 to 6
Outputs:
- mixed: float32 [8, 65536], P('guide', ('kv', 'seq'))
Inputs may be any that keep to these rules, and one draw needn't show every extreme that they name: lengths[0] lies in 1 to 8192 and some request has exactly 8192; lengths[1] lies in 1 to 2048 and some request has exactly 2048. `slot_owner`: each row is a permutation of the 8 requests. `allowed_ids`: the ids of the i-th aligned block of 1024 entries are distinct and lie in rows i * 2048 to (i + 1) * 2048 - 1 of the table.
All inputs are finite; a program needn't handle non-finite values.
Results may differ from a plain program's by a relative error of at most 0.0039.
Values may be sent and summed in bfloat16 or wider, within the bound.
A program may use at most 128 MiB of HBM per device.

v0:
```python
import jax
import jax.numpy as jnp
from jax import lax
from jax.sharding import PartitionSpec as P

D = 4608
H = 32
HD = 128
EPS = 1e-06
ATTN_CAP = 50.0
LOGIT_CAP = 30.0
THETA = 10000.0
HIGHEST = lax.Precision.HIGHEST


def rotary(values, position):
    half_size = values.shape[-1] // 2
    frequency = THETA ** (-2.0 * jnp.arange(half_size, dtype=jnp.float32) / values.shape[-1])
    angles = position[:, None, None] * frequency
    first_half = values[..., :half_size]
    second_half = values[..., half_size:]
    cosine = jnp.cos(angles)
    sine_part = jnp.sin(angles)
    return jnp.concatenate(
        [
            first_half * cosine - second_half * sine_part,
            second_half * cosine + first_half * sine_part,
        ],
        axis=-1,
    )


def to_slots(slot_pick, array):
    flat = array.astype(jnp.float32).reshape(array.shape[0], array.shape[1], -1)
    moved = jnp.einsum("gsr,gre->gse", slot_pick, flat, precision=HIGHEST)
    return moved.reshape(array.shape).astype(array.dtype)


def to_requests(slot_pick, array):
    flat = array.astype(jnp.float32).reshape(array.shape[0], array.shape[1], -1)
    moved = jnp.einsum("gsr,gse->gre", slot_pick, flat, precision=HIGHEST)
    return moved.reshape(array.shape).astype(array.dtype)


def attend_block(queries, key_block, value_block, slot_len, first_pos, tile_len):
    slot_count, block_len = (key_block.shape[0], key_block.shape[1])
    local_kv, group_size, head_size = (queries.shape[1], queries.shape[2], queries.shape[3])
    live_len = jnp.clip(jnp.max(slot_len) - first_pos, 0, block_len)
    tile_count = (live_len + tile_len - 1) // tile_len

    def one_tile(tile_index, carry):
        numer, denom = carry
        tile_start = tile_index * tile_len
        key_tile = key_block.reshape(slot_count, tile_len, local_kv, head_size)
        value_tile = value_block.reshape(slot_count, tile_len, local_kv, head_size)
        scores = jnp.einsum(
            "rkgd,rtkd->rkgt", queries, key_tile, preferred_element_type=jnp.float32
        )
        places = first_pos + tile_start + jnp.arange(tile_len, dtype=jnp.int32)
        visible = places[None, None, None, :] < slot_len[:, None, None, None]
        probs = jnp.where(visible, jnp.exp(ATTN_CAP * jnp.tanh(scores / ATTN_CAP)), 0.0)
        numer = numer + jnp.einsum(
            "rkgt,rtkd->rkgd",
            probs.astype(jnp.bfloat16),
            value_tile,
            preferred_element_type=jnp.float32,
        )
        denom = denom + jnp.sum(probs, axis=-1)
        return (numer, denom)

    start_numer = jnp.zeros((slot_count, local_kv, group_size, head_size), jnp.float32)
    start_denom = jnp.zeros((slot_count, local_kv, group_size), jnp.float32)
    return lax.fori_loop(0, tile_count, one_tile, (start_numer, start_denom))


def on_device(
    hidden,
    lengths,
    slot_owner,
    allowed_ids,
    guidance,
    pre_attn_gain,
    post_attn_gain,
    pre_ffw_gain,
    post_ffw_gain,
    final_gain,
    query_weight,
    key_weight,
    value_weight,
    output_weight,
    gate_weight,
    up_weight,
    down_weight,
    embedding,
    cond_keys,
    cond_values,
    uncond_keys,
    uncond_values,
):
    kinds, requests, width_local = hidden.shape
    stream_count = kinds * requests
    local_heads = query_weight.shape[1] // HD
    local_kv = key_weight.shape[1] // HD
    group_size = local_heads // local_kv
    streams = hidden.astype(jnp.float32)
    normed = (streams * pre_attn_gain).astype(jnp.bfloat16).reshape(stream_count, width_local)
    query_part = jnp.dot(normed, query_weight, preferred_element_type=jnp.float32)
    key_part = jnp.dot(normed, key_weight, preferred_element_type=jnp.float32)
    value_part = jnp.dot(normed, value_weight, preferred_element_type=jnp.float32)
    square_part = jnp.sum(streams * streams, axis=-1)
    square_sum, query_sum, key_sum, value_sum = lax.psum(
        (square_part, query_part, key_part, value_part), ("guide", "seq")
    )
    row_scale = lax.rsqrt(square_sum / D + EPS).reshape(stream_count, 1)
    position = lengths.astype(jnp.float32).reshape(stream_count)
    queries = (
        rotary((query_sum * row_scale).reshape(stream_count, local_heads, HD), position)
        * (D // H) ** (-0.5)
    ).astype(jnp.bfloat16)
    new_keys = rotary((key_sum * row_scale).reshape(stream_count, local_kv, HD), position).astype(
        jnp.bfloat16
    )
    new_values = (value_sum * row_scale).astype(jnp.bfloat16)
    queries = queries.reshape(kinds, requests, local_kv, group_size, HD)
    new_keys = new_keys.reshape(kinds, requests, local_kv, HD)
    new_values = new_values.reshape(kinds, requests, local_kv, HD)
    matches = slot_owner[:, :, None] == jnp.arange(requests, dtype=jnp.int32)[None, None, :]
    slot_pick = matches.astype(jnp.float32)
    slot_len = jnp.sum(jnp.where(matches, lengths[:, None, :], 0), axis=-1)
    slot_queries = to_slots(slot_pick, queries)
    slot_keys = to_slots(slot_pick, new_keys)
    slot_values = to_slots(slot_pick, new_values)
    guide_index = lax.axis_index("guide")
    seq_index = lax.axis_index("seq")
    block_index = guide_index * lax.axis_size("seq") + seq_index
    cond_len = cond_keys.shape[1]
    uncond_len = uncond_keys.shape[1]
    cond_numer, cond_denom = attend_block(
        slot_queries[0],
        cond_keys,
        cond_values,
        slot_len[0],
        block_index * cond_len,
        min(256, cond_len),
    )
    uncond_numer, uncond_denom = attend_block(
        slot_queries[1],
        uncond_keys,
        uncond_values,
        slot_len[1],
        block_index * uncond_len,
        min(256, uncond_len),
    )
    numer_part = jnp.stack([cond_numer, uncond_numer])
    denom_part = jnp.stack([cond_denom, uncond_denom])
    numer_sum, denom_sum = lax.psum((numer_part, denom_part), ("guide", "seq"))
    own_score = jnp.einsum(
        "gskjd,gskd->gskj", slot_queries, slot_keys, preferred_element_type=jnp.float32
    )
    own_prob = jnp.exp(ATTN_CAP * jnp.tanh(own_score / ATTN_CAP))
    own_weight = own_prob.astype(jnp.bfloat16).astype(jnp.float32)
    numer_total = (
        numer_sum + own_weight[..., None] * slot_values.astype(jnp.float32)[:, :, :, None, :]
    )
    denom_total = denom_sum + own_prob
    attended_slots = (numer_total / denom_total[..., None]).astype(jnp.bfloat16)
    attended = to_requests(slot_pick, attended_slots).reshape(stream_count, local_heads * HD)
    out_part = jnp.dot(attended, output_weight, preferred_element_type=jnp.float32)
    projected = lax.psum(out_part, "kv").reshape(kinds, requests, width_local)
    branch_sq = lax.psum(jnp.sum(projected * projected, axis=-1), ("guide", "seq"))
    out_scale = lax.rsqrt(branch_sq / D + EPS)
    middle = streams + projected * out_scale[..., None] * post_attn_gain
    middle_sq = lax.psum(jnp.sum(middle * middle, axis=-1), ("guide", "seq"))
    ffw_in = (middle * pre_ffw_gain).astype(jnp.bfloat16).reshape(stream_count, width_local)
    ffw_scale = lax.rsqrt(middle_sq / D + EPS).reshape(stream_count, 1)
    gate_part = jnp.dot(ffw_in, gate_weight, preferred_element_type=jnp.float32)
    upward_part = jnp.dot(ffw_in, up_weight, preferred_element_type=jnp.float32)
    gate_sum, upward_sum = lax.psum((gate_part, upward_part), ("guide", "seq"))
    activ = (jax.nn.gelu(gate_sum * ffw_scale, approximate=True) * (upward_sum * ffw_scale)).astype(
        jnp.bfloat16
    )
    down_part = jnp.dot(activ, down_weight, preferred_element_type=jnp.float32)
    ffw_out = lax.psum(down_part, "kv").reshape(kinds, requests, width_local)
    ffw_sq = lax.psum(jnp.sum(ffw_out * ffw_out, axis=-1), ("guide", "seq"))
    branch_scale = lax.rsqrt(ffw_sq / D + EPS)
    last = middle + ffw_out * branch_scale[..., None] * post_ffw_gain
    last_sq = lax.psum(jnp.sum(last * last, axis=-1), ("guide", "seq"))
    final_scale = lax.rsqrt(last_sq / D + EPS)
    final_rows = (last * final_gain).astype(jnp.bfloat16)
    half_rows = lax.all_gather(final_rows, "seq", axis=2, tiled=True)
    table_rows = embedding.shape[0]
    block_first = (lax.axis_index("kv") * lax.axis_size("seq") + seq_index) * table_rows
    picked = jnp.take(embedding, allowed_ids - block_first, axis=0)
    logit_part = jnp.einsum(
        "sd,ad->sa",
        half_rows.reshape(stream_count, half_rows.shape[2]),
        picked,
        preferred_element_type=jnp.float32,
    )
    logit_term = jnp.transpose(logit_part.reshape(kinds, requests, picked.shape[0]), (1, 0, 2))
    logit_share = lax.psum_scatter(logit_term, "guide", scatter_dimension=0, tiled=True)
    half_req = requests // 2
    first_req = guide_index * half_req
    share_scale = jnp.transpose(
        lax.dynamic_slice_in_dim(final_scale, first_req, half_req, 1), (1, 0)
    )
    capped = LOGIT_CAP * jnp.tanh(logit_share * share_scale[:, :, None] / LOGIT_CAP)
    share_weight = lax.dynamic_slice_in_dim(guidance, first_req, half_req, 0)
    return capped[:, 1] + share_weight[:, None] * (capped[:, 0] - capped[:, 1])


def solution(mesh):
    return jax.shard_map(
        on_device,
        mesh=mesh,
        in_specs=(
            P(None, None, ("guide", "seq")),
            P(),
            P(),
            P(("kv", "seq")),
            P(),
            P(("guide", "seq")),
            P(("guide", "seq")),
            P(("guide", "seq")),
            P(("guide", "seq")),
            P(("guide", "seq")),
            P(("guide", "seq"), "kv"),
            P(("guide", "seq"), "kv"),
            P(("guide", "seq"), "kv"),
            P("kv", ("guide", "seq")),
            P(("guide", "seq"), "kv"),
            P(("guide", "seq"), "kv"),
            P("kv", ("guide", "seq")),
            P(("kv", "seq"), "guide"),
            P(None, ("guide", "seq"), "kv"),
            P(None, ("guide", "seq"), "kv"),
            P(None, ("guide", "seq"), "kv"),
            P(None, ("guide", "seq"), "kv"),
        ),
        out_specs=P("guide", ("kv", "seq")),
        check_vma=False,
    )
```

profile of v0, /device:TPU:1, one launch (start us, length us, event | category | flops | bytes accessed | tf_op | source)
XLA Modules:
  0.0 685.3 jit_solution(3180978337750881133)
XLA Ops:
  6.5 1.9 fusion.79
  8.5 0.8 fusion.58
  9.3 0.8 select_reduce_fusion
  10.1 0.7 slice_reduce_fusion.1
  10.8 0.7 convert_element_type.96
  11.5 70.0 %psum.99 = f32[2,8]{1,0:T(2,128)S(1)} all-reduce(f32[2,8]{1,0:T(2,128)S(1)} %fusion.58), channel_id=1, replica_groups=mesh['guide'=2,'kv'=4,'seq'=16] {'guide','seq'}, use_global_device_ids=true, to_apply=%region_4.0 | all-reduce | flops 16 | bytes 128 | tf_op jit(solution)/shard_map/psum | solution.py:111
  81.6 1.7 fusion.75
  83.3 1.7 fusion.77
  84.9 0.1 multiply_cosine_fusion
  86.5 23.5 %all-reduce.9.cloned.1.call-done = f32[16,1024]{1,0:T(8,128)} async-done(((f32[16,1024]{1,0:T(8,128)}), f32[16,1024]{1,0:T(8,128)}) %all-reduce.9.cloned.1.call-update) | async-done | bytes 65552 | tf_op jit(solution)/shard_map/psum | solution.py:111
  110.0 0.9 multiply_bitcast_fusion
  110.9 0.1 multiply_subtract_fusion
  111.0 0.1 fusion.49
  111.1 0.9 convolution_convert_fusion.1
  112.0 2.2 fusion.17
  114.3 2.3 while.28
  114.4 2.0 fusion.127
  116.4 0.2 fusion.128
  116.6 0.1 copy.66
  116.7 1.4 fusion.39
  118.2 1.6 while.29
  118.3 1.3 convolution_add_fusion.2
  119.6 0.2 fusion.132
  119.8 0.1 copy.67
  119.9 0.6 pad_maximum_fusion.2
  120.6 0.6 pad_maximum_fusion
  121.3 95.4 %all-reduce.15.cloned.1.call-done = (f32[2,8,4,2]{1,2,3,0:T(4,128)}, f32[16,512]{1,0:T(8,128)}, f32[16,512]{1,0:T(8,128)}) async-done(((f32[2,8,4,2]{1,2,3,0:T(4,128)}, f32[16,512]{1,0:T(8,128)}, f32[16,512]{1,0:T(8,128)}), (f32[2,8,4,2]{1,2,3,0:T(4,128)}, f32[16,512]{1,0:T(8,128)}, f32[16,512]{1,0:T(8,128)})) %all-reduce.15.cloned.1.call-update) | async-done | bytes 66064 | tf_op jit(solution)/shard_map/psum | solution.py:156
  216.7 0.8 broadcast_multiply_fusion
  217.6 0.1 subtract_convert_fusion
  217.7 0.1 pad_maximum_fusion.1
  217.8 0.2 fusion.27
  218.0 0.2 fusion.54
  218.2 0.1 copy.75
  218.3 1.0 fusion.29
  219.3 0.7 fusion.83
  220.0 0.1 copy.63
  220.1 0.1 copy.68
  220.3 93.1 %all-reduce.11.cloned.1.call-done = f32[2,8,4,2,128]{4,3,2,1,0:T(2,128)} async-done(((f32[2,8,4,2,128]{4,3,2,1,0:T(2,128)}), f32[2,8,4,2,128]{4,3,2,1,0:T(2,128)}) %all-reduce.11.cloned.1.call-update) | async-done | bytes 65552 | tf_op jit(solution)/shard_map/psum | solution.py:156
  313.4 1.0 fusion.50
  314.5 0.1 fusion.26
  314.6 0.2 fusion.99
  314.8 13.2 %psum.104 = f32[16,144]{1,0:T(8,128)S(1)} all-reduce(f32[16,144]{1,0:T(8,128)S(1)} %fusion.99), channel_id=1, replica_groups=mesh['guide'=2,'kv'=4,'seq'=16] {'kv'}, use_global_device_ids=true, to_apply=%region_16.17 | all-reduce | flops 2304 | bytes 18432 | tf_op jit(solution)/shard_map/psum | solution.py:169
  327.9 0.1 multiply_reduce_fusion.3
  328.1 67.2 %psum.105 = f32[2,8]{1,0:T(2,128)S(1)} all-reduce(f32[2,8]{1,0:T(2,128)S(1)} %reduce_sum.83), channel_id=1, replica_groups=mesh['guide'=2,'kv'=4,'seq'=16] {'guide','seq'}, use_global_device_ids=true, to_apply=%region_18.19 | all-reduce | flops 16 | bytes 128 | tf_op jit(solution)/shard_map/psum | solution.py:170
  395.4 0.2 multiply_reduce_fusion.2
  395.5 1.3 fusion.89
  396.8 0.5 copy-done.1
  397.3 1.3 fusion.91
  398.7 14.8 %gather_fusion = bf16[1024,2304]{1,0:T(8,128)(2,1)} fusion(bf16[2048,2304]{1,0:T(8,128)(2,1)} %param.43, s32[1024]{0:T(1024)S(1)} %fusion.88), kind=kCustom, calls=%fused_computation | custom fusion | bytes 9441280 | tf_op jit(solution)/shard_map/jit(_take)/gather | solution.py:193
  413.5 0.6 dynamic-slice
  414.7 62.7 %psum.107 = f32[2,8]{1,0:T(2,128)S(1)} all-reduce(f32[2,8]{1,0:T(2,128)S(1)} %get-tuple-element.260), channel_id=1, replica_groups=mesh['guide'=2,'kv'=4,'seq'=16] {'guide','seq'}, use_global_device_ids=true, to_apply=%region_21.22 | all-reduce | flops 16 | bytes 128 | tf_op jit(solution)/shard_map/psum | solution.py:173
  477.5 21.1 %all-reduce.17.cloned.1.call-done = (f32[16,9216]{1,0:T(8,128)}, f32[16,9216]{1,0:T(8,128)}) async-done(((f32[16,9216]{1,0:T(8,128)}, f32[16,9216]{1,0:T(8,128)}), (f32[16,9216]{1,0:T(8,128)}, f32[16,9216]{1,0:T(8,128)})) %all-reduce.17.cloned.1.call-update) | async-done | bytes 1179664 | tf_op jit(solution)/shard_map/psum | solution.py:178
  498.6 3.0 fusion.42
  501.6 13.1 %psum.109 = f32[16,144]{1,0:T(8,128)S(1)} all-reduce(f32[16,144]{1,0:T(8,128)S(1)} %fusion.42), channel_id=1, replica_groups=mesh['guide'=2,'kv'=4,'seq'=16] {'kv'}, use_global_device_ids=true, to_apply=%region_23.24 | all-reduce | flops 2304 | bytes 18432 | tf_op jit(solution)/shard_map/psum | solution.py:183
  514.7 0.1 multiply_reduce_fusion.1
  514.8 0.1 reduce_sum.86
  515.0 69.8 %psum.110 = f32[2,8]{1,0:T(2,128)S(1)} all-reduce(f32[2,8]{1,0:T(2,128)S(1)} %reduce_sum.86), channel_id=1, replica_groups=mesh['guide'=2,'kv'=4,'seq'=16] {'guide','seq'}, use_global_device_ids=true, to_apply=%region_25.26 | all-reduce | flops 16 | bytes 128 | tf_op jit(solution)/shard_map/psum | solution.py:184
  584.8 0.2 multiply_reduce_fusion
  585.0 0.1 copy.69
  585.1 18.4 %all_gather.3 = bf16[2,8,2304]{1,0,2:T(2,128)(2,1)S(1)} all-gather(bf16[2,8,144]{1,0,2:T(2,128)(2,1)S(1)} %copy.69), channel_id=1, replica_groups=mesh['guide'=2,'kv'=4,'seq'=16] {'seq'}, dimensions={2}, use_global_device_ids=true | all-gather | bytes 78336 | tf_op jit(solution)/shard_map/all_gather | solution.py:190
  603.5 4.7 fusion.21
  608.3 68.8 %psum.111 = f32[2,8]{1,0:T(2,128)S(1)} all-reduce(f32[2,8]{1,0:T(2,128)S(1)} %get-tuple-element.266), channel_id=1, replica_groups=mesh['guide'=2,'kv'=4,'seq'=16] {'guide','seq'}, use_global_device_ids=true, to_apply=%region_28.29 | all-reduce | flops 16 | bytes 128 | tf_op jit(solution)/shard_map/psum | solution.py:187
  677.1 0.9 fusion.53
  678.1 0.7 fusion.63
  (65 shorter events, 1.2 us)
Async XLA Ops:
  6.5 389.0 %copy-start = (bf16[144,9216]{1,0:T(8,128)(2,1)S(1)}, bf16[144,9216]{1,0:T(8,128)(2,1)}, u32[]{:S(2)}) copy-start(bf16[144,9216]{1,0:T(8,128)(2,1)} %param.41) | copy-start | bytes 7962628
  6.5 103.4 %all-reduce.9.cloned.1.call-start = ((), (), s32[]{:S(2)}) async-start(), calls=%async_computation | async-start | bytes 131072 | tf_op jit(solution)/shard_map/psum | solution.py:111
  8.5 208.2 %all-reduce.15.cloned.1.call-start = ((), (), s32[]{:S(2)}) async-start(), calls=%async_computation.3 | async-start | bytes 147456 | tf_op jit(solution)/shard_map/psum | solution.py:156
  118.1 99.7 %copy-start.4 = (s32[2,8]{1,0:T(2,128)S(1)}, s32[2,8]{1,0:T(2,128)}, u32[]{:S(2)}) copy-start(s32[2,8]{1,0:T(2,128)} %param.28) | copy-start | bytes 196
  118.1 196.5 %copy-start.2 = (bf16[1024,144]{0,1:T(8,128)(2,1)S(1)}, bf16[1024,144]{0,1:T(8,128)(2,1)}, u32[]{:S(2)}) copy-start(bf16[1024,144]{0,1:T(8,128)(2,1)} %param.39) | copy-start | bytes 884740
  118.1 277.2 %copy-start.3 = (bf16[2,8,144]{2,1,0:T(8,128)(2,1)S(1)}, bf16[2,8,144]{2,1,0:T(8,128)(2,1)}, u32[]{:S(2)}) copy-start(bf16[2,8,144]{2,1,0:T(8,128)(2,1)} %param.26) | copy-start | bytes 13828
  118.2 277.2 %copy-start.7 = (f32[144]{0:T(256)S(1)}, f32[144]{0:T(256)}, u32[]{:S(2)}) copy-start(f32[144]{0:T(256)} %param.32) | copy-start | bytes 1732
  118.2 277.4 %copy-start.6 = (f32[144]{0:T(256)S(1)}, f32[144]{0:T(256)}, u32[]{:S(2)}) copy-start(f32[144]{0:T(256)} %param.33) | copy-start | bytes 1732
  120.5 192.9 %all-reduce.11.cloned.1.call-start = ((), (), s32[]{:S(2)}) async-start(), calls=%async_computation.1 | async-start | bytes 131072 | tf_op jit(solution)/shard_map/psum | solution.py:156
  121.3 377.4 %all-reduce.17.cloned.1.call-start = ((), (), s32[]{:S(2)}) async-start(), calls=%async_computation.4 | async-start | bytes 2359296 | tf_op jit(solution)/shard_map/psum | solution.py:178
  395.3 2.0 copy-start.1
  397.3 1.4 copy-start.5
  398.6 278.5 %all-reduce.13.cloned.1.call-start = ((), (), s32[]{:S(2)}) async-start(), calls=%async_computation.2 | async-start | bytes 131072
  398.7 14.8 %copy-start.11 = (u32[128]{0:T(128)S(1)}, u32[128]{0:T(128)}, u32[]{:S(2)}) copy-start(u32[128]{0:T(128)} %constant.168) | copy-start | bytes 1540
  413.5 101.5 %copy-start.10 = (f32[8]{0:T(128)S(1)}, f32[8]{0:T(128)}, u32[]{:S(2)}) copy-start(f32[8]{0:T(128)} %param.30) | copy-start | bytes 100
  413.5 171.4 %copy-start.8 = (f32[144]{0:T(256)S(1)}, f32[144]{0:T(256)}, u32[]{:S(2)}) copy-start(f32[144]{0:T(256)} %param.34) | copy-start | bytes 1732
  413.5 171.4 %copy-start.9 = (f32[144]{0:T(256)S(1)}, f32[144]{0:T(256)}, u32[]{:S(2)}) copy-start(f32[144]{0:T(256)} %param.35) | copy-start | bytes 1732
Sparse Core Ops, SparseCore 0:
  10.6 99.2 all-reduce.8
  120.6 96.0 all-reduce.14
  220.0 93.3 all-reduce.10
  398.7 99.8 all-reduce.16
  608.4 23.3 all-reduce.12
where the time goes:
time: 686 us; the launch traced here: 685 us
  blocking collectives  383 us (56%)
  waiting for transfers between devices  233 us (34%)
  matrix products  25 us (4%)
  local copies, waits for them, and re-layouts  17.3 us (3%)
  between operations  15.4 us (2%)
  other arithmetic  10.9 us (2%)
    psum x2, waiting for transfers between devices, on_device(): numer_sum, denom_sum = lax.psum((numer_part, denom_part), ('guide', 'seq'))  189 us
    psum x1, blocking collectives, on_device(): lax.psum((square_part, query_part, key_part, value_part), ('guide', 'seq'))  70 us
    psum x1, blocking collectives, on_device(): ffw_sq = lax.psum(jnp.sum(ffw_out * ffw_out, axis=-1), ('guide', 'seq'))  69.8 us
    psum x1, blocking collectives, on_device(): last_sq = lax.psum(jnp.sum(last * last, axis=-1), ('guide', 'seq'))  68.8 us
    psum x1, blocking collectives, on_device(): lax.psum(jnp.sum(projected * projected, axis=-1), ('guide', 'seq'))  67.2 us
    psum x1, blocking collectives, on_device(): middle_sq = lax.psum(jnp.sum(middle * middle, axis=-1), ('guide', 'seq'))  62.7 us
    psum x1, waiting for transfers between devices, on_device(): lax.psum((square_part, query_part, key_part, value_part), ('guide', 'seq'))  23.5 us
    psum x1, waiting for transfers between devices, on_device(): gate_sum, upward_sum = lax.psum((gate_part, upward_part), ('guide', 'seq'))  21.1 us
  transfers between devices with their start and end apart: 5, of which 4 were waited for; matrix products, arithmetic and copies ran while one was open for 4% of the time, Pallas kernels for 0%

commit v1 on v0

--- a/solution.py
+++ b/solution.py
@@ -181,7 +181,7 @@
     )
     down_part = jnp.dot(activ, down_weight, preferred_element_type=jnp.float32)
     ffw_out = lax.psum(down_part, "kv").reshape(kinds, requests, width_local)
-    ffw_sq = lax.psum(jnp.sum(ffw_out * ffw_out, axis=-1), ("guide", "seq"))
+    ffw_sq = lax.psum(lax.psum(jnp.sum(ffw_out * ffw_out, axis=-1), "guide"), "seq")
     branch_scale = lax.rsqrt(ffw_sq / D + EPS)
     last = middle + ffw_out * branch_scale[..., None] * post_ffw_gain
     last_sq = lax.psum(jnp.sum(last * last, axis=-1), ("guide", "seq"))

time: 686 us -> 662 us (0.965)
  blocking collectives: 383 us -> 359 us
    psum x1 -> x2, blocking collectives: 69.8 us -> 37.9 us  [the longest x1 31.2 us: on_device(): lax.psum(lax.psum(jnp.sum(ffw_out * ffw_out, axis=-1), 'guide'), 'seq')]
    psum x1, blocking collectives: 68.8 us -> 77.5 us  [on_device(): last_sq = lax.psum(jnp.sum(last * last, axis=-1), ('guide', 'seq'))]
where the time goes in v1:
time: 662 us; the launch traced here: 661 us
  blocking collectives  359 us (54%)
  waiting for transfers between devices  233 us (35%)
  matrix products  25 us (4%)
  local copies, waits for them, and re-layouts  17.3 us (3%)
  between operations  15.4 us (2%)
  other arithmetic  10.9 us (2%)
    psum x2, waiting for transfers between devices, on_device(): numer_sum, denom_sum = lax.psum((numer_part, denom_part), ('guide', 'seq'))  189 us
    psum x1, blocking collectives, on_device(): last_sq = lax.psum(jnp.sum(last * last, axis=-1), ('guide', 'seq'))  77.5 us
    psum x1, blocking collectives, on_device(): lax.psum((square_part, query_part, key_part, value_part), ('guide', 'seq'))  70 us
    psum x1, blocking collectives, on_device(): lax.psum(jnp.sum(projected * projected, axis=-1), ('guide', 'seq'))  67.2 us
    psum x1, blocking collectives, on_device(): middle_sq = lax.psum(jnp.sum(middle * middle, axis=-1), ('guide', 'seq'))  62.7 us
    psum x1, blocking collectives, on_device(): lax.psum(lax.psum(jnp.sum(ffw_out * ffw_out, axis=-1), 'guide'), 'seq')  31.2 us
    psum x1, waiting for transfers between devices, on_device(): lax.psum((square_part, query_part, key_part, value_part), ('guide', 'seq'))  23.5 us
    psum x1, waiting for transfers between devices, on_device(): gate_sum, upward_sum = lax.psum((gate_part, upward_part), ('guide', 'seq'))  21.1 us
  transfers between devices with their start and end apart: 5, of which 4 were waited for; matrix products, arithmetic and copies ran while one was open for 4% of the time, Pallas kernels for 0%

profile of v1, /device:TPU:1, one launch (start us, length us, event | category | flops | bytes accessed | tf_op | source)
XLA Modules:
  0.0 660.7 jit_solution(10040463177916243153)
XLA Ops:
  6.5 1.9 fusion.79
  8.5 0.8 fusion.58
  9.3 0.8 select_reduce_fusion
  10.1 0.7 slice_reduce_fusion.1
  10.8 0.7 convert_element_type.96
  11.5 70.0 %psum.106 = f32[2,8]{1,0:T(2,128)S(1)} all-reduce(f32[2,8]{1,0:T(2,128)S(1)} %fusion.58), channel_id=1, replica_groups=mesh['guide'=2,'kv'=4,'seq'=16] {'guide','seq'}, use_global_device_ids=true, to_apply=%region_4.0 | all-reduce | flops 16 | bytes 128 | tf_op jit(solution)/shard_map/psum | solution.py:111
  81.6 1.7 fusion.75
  83.3 1.7 fusion.77
  84.9 0.1 multiply_cosine_fusion
  86.5 23.5 %all-reduce.9.cloned.1.call-done = f32[16,1024]{1,0:T(8,128)} async-done(((f32[16,1024]{1,0:T(8,128)}), f32[16,1024]{1,0:T(8,128)}) %all-reduce.9.cloned.1.call-update) | async-done | bytes 65552 | tf_op jit(solution)/shard_map/psum | solution.py:111
  110.0 0.9 multiply_bitcast_fusion
  110.9 0.1 multiply_subtract_fusion
  111.0 0.1 fusion.49
  111.1 0.9 convolution_convert_fusion.1
  112.0 2.2 fusion.17
  114.3 2.3 while.28
  114.4 2.0 fusion.127
  116.4 0.2 fusion.128
  116.6 0.1 copy.66
  116.7 1.4 fusion.39
  118.2 1.6 while.29
  118.3 1.3 convolution_add_fusion.2
  119.6 0.2 fusion.132
  119.8 0.1 copy.67
  119.9 0.6 pad_maximum_fusion.2
  120.6 0.6 pad_maximum_fusion
  121.3 95.4 %all-reduce.15.cloned.1.call-done = (f32[2,8,4,2]{1,2,3,0:T(4,128)}, f32[16,512]{1,0:T(8,128)}, f32[16,512]{1,0:T(8,128)}) async-done(((f32[2,8,4,2]{1,2,3,0:T(4,128)}, f32[16,512]{1,0:T(8,128)}, f32[16,512]{1,0:T(8,128)}), (f32[2,8,4,2]{1,2,3,0:T(4,128)}, f32[16,512]{1,0:T(8,128)}, f32[16,512]{1,0:T(8,128)})) %all-reduce.15.cloned.1.call-update) | async-done | bytes 66064 | tf_op jit(solution)/shard_map/psum | solution.py:156
  216.7 0.8 broadcast_multiply_fusion
  217.6 0.1 subtract_convert_fusion
  217.7 0.1 pad_maximum_fusion.1
  217.8 0.2 fusion.27
  218.0 0.2 fusion.54
  218.2 0.1 copy.75
  218.3 1.0 fusion.29
  219.3 0.7 fusion.83
  220.0 0.1 copy.63
  220.1 0.1 copy.68
  220.3 93.1 %all-reduce.11.cloned.1.call-done = f32[2,8,4,2,128]{4,3,2,1,0:T(2,128)} async-done(((f32[2,8,4,2,128]{4,3,2,1,0:T(2,128)}), f32[2,8,4,2,128]{4,3,2,1,0:T(2,128)}) %all-reduce.11.cloned.1.call-update) | async-done | bytes 65552 | tf_op jit(solution)/shard_map/psum | solution.py:156
  313.4 1.0 fusion.50
  314.5 0.1 fusion.26
  314.6 0.2 fusion.99
  314.8 13.2 %psum.111 = f32[16,144]{1,0:T(8,128)S(1)} all-reduce(f32[16,144]{1,0:T(8,128)S(1)} %fusion.99), channel_id=1, replica_groups=mesh['guide'=2,'kv'=4,'seq'=16] {'kv'}, use_global_device_ids=true, to_apply=%region_16.17 | all-reduce | flops 2304 | bytes 18432 | tf_op jit(solution)/shard_map/psum | solution.py:169
  327.9 0.1 multiply_reduce_fusion.3
  328.1 67.2 %psum.112 = f32[2,8]{1,0:T(2,128)S(1)} all-reduce(f32[2,8]{1,0:T(2,128)S(1)} %reduce_sum.83), channel_id=1, replica_groups=mesh['guide'=2,'kv'=4,'seq'=16] {'guide','seq'}, use_global_device_ids=true, to_apply=%region_18.19 | all-reduce | flops 16 | bytes 128 | tf_op jit(solution)/shard_map/psum | solution.py:170
  395.4 0.2 multiply_reduce_fusion.2
  395.5 1.3 fusion.89
  396.8 0.5 copy-done.1
  397.3 1.3 fusion.91
  398.7 14.8 %gather_fusion = bf16[1024,2304]{1,0:T(8,128)(2,1)} fusion(bf16[2048,2304]{1,0:T(8,128)(2,1)} %param.43, s32[1024]{0:T(1024)S(1)} %fusion.88), kind=kCustom, calls=%fused_computation | custom fusion | bytes 9441280 | tf_op jit(solution)/shard_map/jit(_take)/gather | solution.py:193
  413.5 0.6 dynamic-slice
  414.7 62.7 %psum.114 = f32[2,8]{1,0:T(2,128)S(1)} all-reduce(f32[2,8]{1,0:T(2,128)S(1)} %get-tuple-element.260), channel_id=1, replica_groups=mesh['guide'=2,'kv'=4,'seq'=16] {'guide','seq'}, use_global_device_ids=true, to_apply=%region_21.22 | all-reduce | flops 16 | bytes 128 | tf_op jit(solution)/shard_map/psum | solution.py:173
  477.5 21.1 %all-reduce.17.cloned.1.call-done = (f32[16,9216]{1,0:T(8,128)}, f32[16,9216]{1,0:T(8,128)}) async-done(((f32[16,9216]{1,0:T(8,128)}, f32[16,9216]{1,0:T(8,128)}), (f32[16,9216]{1,0:T(8,128)}, f32[16,9216]{1,0:T(8,128)})) %all-reduce.17.cloned.1.call-update) | async-done | bytes 1179664 | tf_op jit(solution)/shard_map/psum | solution.py:178
  498.6 3.0 fusion.42
  501.6 13.1 %psum.116 = f32[16,144]{1,0:T(8,128)S(1)} all-reduce(f32[16,144]{1,0:T(8,128)S(1)} %fusion.42), channel_id=1, replica_groups=mesh['guide'=2,'kv'=4,'seq'=16] {'kv'}, use_global_device_ids=true, to_apply=%region_23.24 | all-reduce | flops 2304 | bytes 18432 | tf_op jit(solution)/shard_map/psum | solution.py:183
  514.7 0.1 multiply_reduce_fusion.1
  514.9 6.7 %psum.117 = f32[2,8]{1,0:T(2,128)S(1)} all-reduce(f32[2,8]{1,0:T(2,128)S(1)} %reduce_sum.86), channel_id=1, replica_groups=mesh['guide'=2,'kv'=4,'seq'=16] {'guide'}, use_global_device_ids=true, to_apply=%region_25.26 | all-reduce | flops 16 | bytes 128 | tf_op jit(solution)/shard_map/psum | solution.py:184
  521.7 31.2 %psum.118 = f32[2,8]{1,0:T(2,128)S(1)} all-reduce(f32[2,8]{1,0:T(2,128)S(1)} %psum.117), channel_id=1, replica_groups=mesh['guide'=2,'kv'=4,'seq'=16] {'seq'}, use_global_device_ids=true, to_apply=%region_26.27 | all-reduce | flops 16 | bytes 128 | tf_op jit(solution)/shard_map/psum | solution.py:184
  552.9 0.2 multiply_reduce_fusion
  553.0 0.1 copy.69
  553.2 17.0 %all_gather.3 = bf16[2,8,2304]{1,0,2:T(2,128)(2,1)S(1)} all-gather(bf16[2,8,144]{1,0,2:T(2,128)(2,1)S(1)} %copy.69), channel_id=1, replica_groups=mesh['guide'=2,'kv'=4,'seq'=16] {'seq'}, dimensions={2}, use_global_device_ids=true | all-gather | bytes 78336 | tf_op jit(solution)/shard_map/all_gather | solution.py:190
  570.2 4.7 fusion.21
  575.0 77.5 %psum.119 = f32[2,8]{1,0:T(2,128)S(1)} all-reduce(f32[2,8]{1,0:T(2,128)S(1)} %get-tuple-element.266), channel_id=1, replica_groups=mesh['guide'=2,'kv'=4,'seq'=16] {'guide','seq'}, use_global_device_ids=true, to_apply=%region_29.30 | all-reduce | flops 16 | bytes 128 | tf_op jit(solution)/shard_map/psum | solution.py:187
  652.5 0.9 fusion.53
  653.5 0.7 fusion.63
  (66 shorter events, 1.3 us)
Async XLA Ops:
  6.5 389.0 %copy-start = (bf16[144,9216]{1,0:T(8,128)(2,1)S(1)}, bf16[144,9216]{1,0:T(8,128)(2,1)}, u32[]{:S(2)}) copy-start(bf16[144,9216]{1,0:T(8,128)(2,1)} %param.41) | copy-start | bytes 7962628
  6.5 103.4 %all-reduce.9.cloned.1.call-start = ((), (), s32[]{:S(2)}) async-start(), calls=%async_computation | async-start | bytes 131072 | tf_op jit(solution)/shard_map/psum | solution.py:111
  8.5 208.2 %all-reduce.15.cloned.1.call-start = ((), (), s32[]{:S(2)}) async-start(), calls=%async_computation.3 | async-start | bytes 147456 | tf_op jit(solution)/shard_map/psum | solution.py:156
  118.1 99.7 %copy-start.4 = (s32[2,8]{1,0:T(2,128)S(1)}, s32[2,8]{1,0:T(2,128)}, u32[]{:S(2)}) copy-start(s32[2,8]{1,0:T(2,128)} %param.28) | copy-start | bytes 196
  118.1 196.5 %copy-start.2 = (bf16[1024,144]{0,1:T(8,128)(2,1)S(1)}, bf16[1024,144]{0,1:T(8,128)(2,1)}, u32[]{:S(2)}) copy-start(bf16[1024,144]{0,1:T(8,128)(2,1)} %param.39) | copy-start | bytes 884740
  118.1 277.2 %copy-start.3 = (bf16[2,8,144]{2,1,0:T(8,128)(2,1)S(1)}, bf16[2,8,144]{2,1,0:T(8,128)(2,1)}, u32[]{:S(2)}) copy-start(bf16[2,8,144]{2,1,0:T(8,128)(2,1)} %param.26) | copy-start | bytes 13828
  118.2 277.2 %copy-start.7 = (f32[144]{0:T(256)S(1)}, f32[144]{0:T(256)}, u32[]{:S(2)}) copy-start(f32[144]{0:T(256)} %param.32) | copy-start | bytes 1732
  118.2 277.4 %copy-start.6 = (f32[144]{0:T(256)S(1)}, f32[144]{0:T(256)}, u32[]{:S(2)}) copy-start(f32[144]{0:T(256)} %param.33) | copy-start | bytes 1732
  120.5 192.9 %all-reduce.11.cloned.1.call-start = ((), (), s32[]{:S(2)}) async-start(), calls=%async_computation.1 | async-start | bytes 131072 | tf_op jit(solution)/shard_map/psum | solution.py:156
  121.3 377.4 %all-reduce.17.cloned.1.call-start = ((), (), s32[]{:S(2)}) async-start(), calls=%async_computation.4 | async-start | bytes 2359296 | tf_op jit(solution)/shard_map/psum | solution.py:178
  395.3 2.0 copy-start.1
  397.3 1.4 copy-start.5
  398.6 253.9 %all-reduce.13.cloned.1.call-start = ((), (), s32[]{:S(2)}) async-start(), calls=%async_computation.2 | async-start | bytes 131072
  398.7 14.8 %copy-start.11 = (u32[128]{0:T(128)S(1)}, u32[128]{0:T(128)}, u32[]{:S(2)}) copy-start(u32[128]{0:T(128)} %constant.168) | copy-start | bytes 1540
  413.5 108.1 %copy-start.10 = (f32[8]{0:T(128)S(1)}, f32[8]{0:T(128)}, u32[]{:S(2)}) copy-start(f32[8]{0:T(128)} %param.30) | copy-start | bytes 100
  413.5 139.4 %copy-start.8 = (f32[144]{0:T(256)S(1)}, f32[144]{0:T(256)}, u32[]{:S(2)}) copy-start(f32[144]{0:T(256)} %param.34) | copy-start | bytes 1732
  413.5 139.4 %copy-start.9 = (f32[144]{0:T(256)S(1)}, f32[144]{0:T(256)}, u32[]{:S(2)}) copy-start(f32[144]{0:T(256)} %param.35) | copy-start | bytes 1732
Sparse Core Ops, SparseCore 0:
  10.6 99.2 all-reduce.8
  120.6 96.0 all-reduce.14
  220.0 93.3 all-reduce.10
  398.7 99.8 all-reduce.16
  575.1 32.9 all-reduce.12
